TPU v7x, 32 devices: a whole 2x2x4 slice. The times are simulated.
32 devices in a mesh: dp: 4 (over y, x), seq: 8 (over z, core).
Axes of the slice: x: 2, y: 2, z: 4, core: 2. Of those that a mesh axis runs over, the one named last changes fastest.
Arguments:
- student_x: bfloat16 [4096, 4096], P(('dp', 'seq')), parts along dimension 0, may hold values from -60 to 60
- student_z: bfloat16 [4096, 4096], P(('dp', 'seq')), parts along dimension 0, may hold values from -6 to 6
- student_b: bfloat16 [4096, 1024], P(('dp', 'seq')), parts along dimension 0, may hold values from -0.5 to 0.5
- student_c: bfloat16 [4096, 1024], P(('dp', 'seq')), parts along dimension 0, may hold values from -6 to 6
- step_size: float32 [64, 4096], P(None, ('dp', 'seq')), parts along dimension 1, may hold values from 0 to 1
- decay_rate: float32 [64], replicated, may hold values from 0.5 to 2
- norm_gain: float32 [4096], replicated, may hold values from 0.5 to 1.5
- teacher_q: bfloat16 [4096, 4096], P(('dp', 'seq')), parts along dimension 0, may hold values from -140 to 140
- teacher_k: bfloat16 [4096, 1024], P(('dp', 'seq')), parts along dimension 0, may hold values from -7 to 7
- teacher_v: bfloat16 [4096, 1024], P(('dp', 'seq')), parts along dimension 0, may hold values from -6 to 6
Outputs:
- student_out: bfloat16 [4096, 4096], P(('dp', 'seq')), parts along dimension 0
- teacher_out: bfloat16 [4096, 4096], P(('dp', 'seq')), parts along dimension 0
There are 4 independent parts, one for each index of `dp`. A program takes and returns all parts, laid end to end along the dimension named above; an argument that names none is the same for every part. Nothing has to cross between parts.
All inputs are finite; a program needn't handle non-finite values.
Results may differ from a plain program's by a relative error of at most 0.0075.
Values may be sent and summed in bfloat16 or wider, within the bound.
A program may use at most 256 MiB of HBM per device.

v0:
```python
import math

import jax
import jax.numpy as jnp
from jax import lax
from jax.sharding import PartitionSpec as P

GROUPS = 8
HEAD_SIZE = 128
BLOCK = 128


epsilon_norm = 1e-05
masked_score = -1e30
HIGHEST = lax.Precision.HIGHEST


def entering(array, axis, combine, identity):
    devices, place = (lax.axis_size(axis), lax.axis_index(axis))
    everything = jax.tree.map(
        lambda part, kind: lax.all_gather(part.astype(kind), axis),
        array,
        (jnp.bfloat16, jnp.bfloat16),
    )
    start = jax.tree.map(
        lambda part, zero: jnp.broadcast_to(jnp.asarray(zero, part.dtype), part.shape),
        array,
        identity,
    )

    def step(k, before):
        reached = k < place
        new = combine(
            before, jax.tree.map(lambda part, own: part[k].astype(own.dtype), everything, array)
        )
        return jax.tree.map(lambda a, b: jnp.where(reached, a, b), new, before)

    return lax.fori_loop(0, devices, step, start)


def block_pass(carry_state, block_inputs, decay_rate, group_count):
    x_block, b_block, c_block, step_block = block_inputs
    block_rows = x_block.shape[0]
    head_count = step_block.shape[0]
    state_dim = b_block.shape[1] // group_count
    per_group = head_count // group_count
    head_width = x_block.shape[1] // head_count
    log_decay = -step_block * decay_rate[:, None]
    running = jnp.cumsum(log_decay, axis=1)
    b_three = b_block.reshape(block_rows, group_count, state_dim)
    c_three = c_block.reshape(block_rows, group_count, state_dim)
    x_four = x_block.reshape(block_rows, group_count, per_group, head_width)
    products = jnp.einsum("tgn,sgn->gts", c_three, b_three, preferred_element_type=jnp.float32)
    lower_mask = jnp.arange(block_rows)[:, None] >= jnp.arange(block_rows)[None, :]
    spread = running[:, :, None] - running[:, None, :]
    factor = jnp.exp(jnp.where(lower_mask[None], spread, masked_score))
    weights = (
        products[:, None] * factor.reshape(group_count, per_group, block_rows, block_rows)
    ).astype(jnp.bfloat16)
    local_out = jnp.einsum("gkts,sgkp->tgkp", weights, x_four, preferred_element_type=jnp.float32)
    state_four = carry_state.reshape(group_count, per_group, head_width, state_dim)
    carried = jnp.einsum(
        "tgn,gkpn->tgkp", c_three.astype(jnp.float32), state_four, precision=HIGHEST
    )
    carried = carried * jnp.exp(running).T.reshape(block_rows, group_count, per_group, 1)
    tail_decay = jnp.exp(running[:, -1:] - running)
    scaled = x_four.astype(jnp.float32) * tail_decay.T.reshape(
        block_rows, group_count, per_group, 1
    )
    fresh_state = jnp.einsum(
        "sgkp,sgn->gkpn", scaled, b_three.astype(jnp.float32), precision=HIGHEST
    )
    new_state = (
        jnp.exp(running[:, -1]).reshape(group_count, per_group, 1, 1) * state_four + fresh_state
    )
    combined = (local_out + carried).reshape(block_rows, head_count * head_width)
    return (new_state.reshape(head_count, head_width, state_dim), combined)


def attend_block(fold_carry, query_four, key_block, value_block, key_start, query_pos, score_scale):
    row_max, row_total, weighted = fold_carry
    key_rows = key_block.shape[0]
    kv_count = query_four.shape[1]
    head_width = query_four.shape[3]
    keys_three = key_block.reshape(key_rows, kv_count, head_width)
    values_three = value_block.reshape(key_rows, kv_count, head_width)
    scores = (
        jnp.einsum("qgkd,sgd->qgks", query_four, keys_three, preferred_element_type=jnp.float32)
        * score_scale
    )
    key_pos = key_start + jnp.arange(key_rows)
    visible = (key_pos[None, :] <= query_pos[:, None])[:, None, None, :]
    masked = jnp.where(visible, scores, masked_score)
    new_max = jnp.maximum(row_max, jnp.max(masked, axis=3))
    shrink = jnp.exp(row_max - new_max)
    probabilities = jnp.where(visible, jnp.exp(masked - new_max[..., None]), 0.0)
    row_total = row_total * shrink + jnp.sum(probabilities, axis=3)
    update = jnp.einsum(
        "qgks,sgd->qgkd",
        probabilities.astype(jnp.bfloat16),
        values_three,
        preferred_element_type=jnp.float32,
    )
    weighted = weighted * shrink[..., None] + update
    return (new_max, row_total, weighted)


def on_device(
    student_x,
    student_z,
    student_b,
    student_c,
    step_size,
    decay_rate,
    norm_gain,
    teacher_q,
    teacher_k,
    teacher_v,
):
    tokens, width = student_x.shape
    head_count = step_size.shape[0]
    head_width = width // head_count
    group_count = GROUPS
    per_group = head_count // group_count
    state_dim = student_b.shape[1] // group_count
    block_count = tokens // BLOCK
    my_index = lax.axis_index("seq")
    blocks_in = (
        student_x.reshape(block_count, BLOCK, width),
        student_b.reshape(block_count, BLOCK, group_count * state_dim),
        student_c.reshape(block_count, BLOCK, group_count * state_dim),
        step_size.reshape(head_count, block_count, BLOCK).transpose(1, 0, 2),
    )

    def advance(carry_state, block_inputs):
        return block_pass(carry_state, block_inputs, decay_rate, group_count)

    zero_state = jnp.zeros((head_count, head_width, state_dim), jnp.float32)
    local_state, block_outs = lax.scan(advance, zero_state, blocks_in)
    cum_device = jnp.cumsum(-step_size * decay_rate[:, None], axis=1)
    device_decay = jnp.exp(cum_device[:, -1])

    def combine(earlier, following):
        return (earlier[0] * following[0], following[0][:, None, None] * earlier[1] + following[1])

    identity = (jnp.ones_like(device_decay), jnp.zeros_like(local_state))
    incoming = entering((device_decay, local_state), "seq", combine, identity)[1]
    ratio = teacher_q.shape[1] // teacher_k.shape[1]
    kv_count = teacher_k.shape[1] // HEAD_SIZE
    query_four = teacher_q.reshape(tokens, kv_count, ratio, HEAD_SIZE)
    query_pos = my_index * tokens + jnp.arange(tokens)
    score_scale = 1.0 / math.sqrt(HEAD_SIZE)
    start_carry = (
        jnp.full((tokens, kv_count, ratio), masked_score, jnp.float32),
        jnp.zeros((tokens, kv_count, ratio), jnp.float32),
        jnp.zeros((tokens, kv_count, ratio, HEAD_SIZE), jnp.float32),
    )
    key_piece = lax.all_gather(teacher_k, "seq", axis=0, tiled=True)
    value_piece = lax.all_gather(teacher_v, "seq", axis=0, tiled=True)
    piece_rows = key_piece.shape[0]
    sub_rows = math.gcd(piece_rows, 512)

    def visit_block(block_index, current):
        key_block = lax.dynamic_slice_in_dim(key_piece, block_index * sub_rows, sub_rows, 0)
        value_block = lax.dynamic_slice_in_dim(value_piece, block_index * sub_rows, sub_rows, 0)
        return attend_block(
            current,
            query_four,
            key_block,
            value_block,
            block_index * sub_rows,
            query_pos,
            score_scale,
        )

    final_carry = lax.fori_loop(0, piece_rows // sub_rows, visit_block, start_carry)
    _, row_total, weighted = final_carry
    teacher_out = (
        (weighted / row_total[..., None])
        .reshape(tokens, kv_count * ratio * HEAD_SIZE)
        .astype(jnp.bfloat16)
    )
    c_three = student_c.reshape(tokens, group_count, state_dim).astype(jnp.float32)
    in_four = incoming.reshape(group_count, per_group, head_width, state_dim)
    carried_in = jnp.einsum("tgn,gkpn->tgkp", c_three, in_four, precision=HIGHEST)
    carried_in = carried_in * jnp.exp(cum_device).T.reshape(tokens, group_count, per_group, 1)
    combined = block_outs.reshape(tokens, group_count, per_group, head_width) + carried_in
    gated_out = combined.reshape(tokens, head_count, head_width) * jax.nn.silu(
        student_z.astype(jnp.float32)
    ).reshape(tokens, head_count, head_width)
    mean_square = jnp.mean(gated_out * gated_out, axis=2, keepdims=True)
    normed = (
        gated_out
        * lax.rsqrt(mean_square + epsilon_norm)
        * norm_gain.reshape(1, head_count, head_width)
    )
    student_out = normed.reshape(tokens, width).astype(jnp.bfloat16)
    return (student_out, teacher_out)


def solution(mesh):
    return jax.shard_map(
        on_device,
        mesh=mesh,
        in_specs=(
            P(("dp", "seq"), None),
            P(("dp", "seq"), None),
            P(("dp", "seq"), None),
            P(("dp", "seq"), None),
            P(None, ("dp", "seq")),
            P(),
            P(),
            P(("dp", "seq"), None),
            P(("dp", "seq"), None),
            P(("dp", "seq"), None),
        ),
        out_specs=(P(("dp", "seq"), None), P(("dp", "seq"), None)),
        check_vma=False,
    )
```

profile of v0, /device:TPU:0, one launch (start us, length us, event | category | flops | bytes accessed | tf_op | source)
XLA Modules:
  0.0 190.1 jit_solution(6066163782654913500)
XLA Ops:
  7.2 1.9 copy.44
  9.2 1.8 copy.46
  13.3 2.2 %add_convert_fusion = bf16[8,8,64,128]{3,2,1,0:T(8,128)(2,1)} fusion(bf16[128,8,8,64]{0,3,2,1:T(8,128)(2,1)S(1)} %bitcast.130, f32[128,8,8]{0,2,1:T(8,128)S(1)} %get-tuple-element.366, f32[8,8]{1,0:T(8,128)S(1)} %mul.192, bf16[128,8,128,1]{2,1,0,3:T(8,128)(2,1)S(1)} %bitcast.135), kind=kOutput, calls=%fused_computation.42 | convolution fusion | flops 807403520 | bytes 2392320 | tf_op jit(solution)/shard_map/while/body/eval_jaxpr/sgkp,sgn->gkpn/dot_general | solution.py:70
  17.3 19.1 %all-reduce = bf16[512]{0:T(512)(128)(2,1)S(1)} all-reduce(bf16[512]{0:T(512)(128)(2,1)S(1)} %dynamic-update-slice), channel_id=2, replica_groups=mesh['dp'=4,'seq'=8] {'seq'}, use_global_device_ids=true, to_apply=%add | all-reduce | flops 512 | bytes 2048
  39.4 2.3 %copy.45 = bf16[128,4096]{0,1:T(8,128)(2,1)} copy(bf16[128,4096]{1,0:T(8,128)(2,1)} %param.21) | data formatting | bytes 2097152 | tf_op args[7]
  44.8 2.3 %fusion.34 = f32[8,8,64,128]{3,2,1,0:T(8,128)} fusion(bf16[128,8,128,1]{2,1,0,3:T(8,128)(2,1)S(1)} %bitcast.127), kind=kOutput, calls=%fused_computation.52 | convolution fusion | flops 805306368 | bytes 2359296 | tf_op jit(solution)/shard_map/while/body/eval_jaxpr/tgn,gkpn->tgkp/dot_general | solution.py:62
  47.1 3.2 %fusion.18 = f32[8,8,128,64]{2,3,1,0:T(8,128)} fusion(bf16[128,8,8,64]{0,3,2,1:T(8,128)(2,1)S(1)} %bitcast.131, f32[8,8,128]{2,1,0:T(8,128)S(1)} %bitcast.134, f32[8,128,128]{2,1,0:T(8,128)S(1)} %fusion.36, pred[128,128]{1,0:T(8,128)(4,1)S(1)} %iota_compare_fusion), kind=kOutput, calls=%fused_computation.31 | convolution fusion | flops 138412032 | bytes 3719168 | tf_op jit(solution)/shard_map/while/body/eval_jaxpr/gkts,sgkp->tgkp/dot_general | solution.py:60
  50.4 24.1 %all-gather.9.cloned.1.call-done = bf16[1024,1024]{0,1:T(8,128)(2,1)} async-done(((bf16[128,1024]{0,1:T(8,128)(2,1)}), bf16[1024,1024]{0,1:T(8,128)(2,1)}) %all-gather.9.cloned.1.call-update) | async-done | bytes 2097168 | tf_op jit(solution)/shard_map/all_gather | solution.py:159
  74.5 37.5 %while.38 = (s32[]{:T(128)}, f32[128,8,4]{0,2,1:T(4,128)S(1)}, f32[128,8,4]{0,2,1:T(4,128)S(1)}, f32[128,8,4,128]{0,3,2,1:T(8,128)}, bf16[1024,1024]{0,1:T(8,128...) while((s32[]{:T(128)}, f32[128,8,4]{0,2,1:T(4,128)S(1)}, ...), condition=%wide.region_7.8_spmd.clone, body=%wide.region_4.7_spmd.clone.sunk | while | flops 1102664320 | bytes 70784216 | solution.py:176
  74.5 2.6 %constant_dynamic-slice_fusion.3 = (bf16[512,1024]{0,1:T(8,128)(2,1)}, bf16[512,1024]{0,1:T(8,128)(2,1)S(1)}) fusion(bf16[1024,1024]{0,1:T(8,128)(2,1)} %get-tuple-element.512, s32[]{:T(128)S(6)} %select_n.96, bf16[1024,1024]{0,1:T(8,128)(2,1)} %get-tuple-element.510), kind=kLoop, calls=%fused_computation.20.clone.1 | loop fusion | bytes 4194308 | tf_op jit(solution)/shard_map/while/body/eval_jaxpr/dynamic_slice | solution.py:165
  77.3 4.7 %fusion.68 = (f32[128,8,4]{0,2,1:T(4,128)S(1)}, f32[8,512,128,4]{2,1,3,0:T(8,128)}) fusion(pred[128,512]{0,1:T(8,128)(4,1)S(1)} %broadcast_compare_fusion.2, bf16[512,8,128,1]{0,2,3,1:T(8,128)(2,1)S(1)} %bitcast.122, bf16[128,8,4,128]{3,0,2,1:T(8,128)(2,1)S(1)} %get-tuple-element.511), kind=kOutput, calls=%fused_computation.6.clone.1 | convolution fusion | flops 543158272 | bytes 10567680 | tf_op jit(solution)/shard_map/while/body/eval_jaxpr/qgkd,sgd->qgks/dot_general | solution.py:88
  82.0 5.7 %fusion.69 = f32[128,8,4]{0,2,1:T(4,128)S(1)} fusion(f32[8,512,128,4]{2,1,3,0:T(8,128)} %get-tuple-element.457, f32[128,8,4]{0,2,1:T(4,128)S(1)} %select_maximum_fusion.2, pred[128,512]{0,1:T(8,128)(4,1)S(1)} %broadcast_compare_fusion.2), kind=kLoop, calls=%fused_computation.8.clone.1 | loop fusion | flops 10481664 | bytes 8486912 | tf_op jit(solution)/shard_map/while/body/eval_jaxpr/reduce_sum | solution.py:97
  88.9 4.6 %bitcast_add_fusion.2 = f32[128,8,4,128]{0,3,2,1:T(8,128)} fusion(f32[128,8,4,128]{0,3,2,1:T(8,128)} %get-tuple-element.497, bf16[512,8,128,1]{0,2,3,1:T(8,128)(2,1)} %bitcast.124, f32[8,512,128,4]{2,1,3,0:T(8,128)S(1)} %copy-done, f32[128,8,4]{0,2,1:T(4,128)S(1)} %select_maximum_fusion.2, pred[128,512]{0,1:T(8,128)(4,1)S(1)} %broadcast_compare_fusion.2, ...), kind=kOutput, calls=%fused_computation.11.clone.1 | convolution fusion | flops 548929536 | bytes 13729793 | tf_op jit(solution)/shard_map/while/body/eval_jaxpr/qgks,sgd->qgkd/dot_general | solution.py:98
  93.5 2.6 %constant_dynamic-slice_fusion.3 = (bf16[512,1024]{0,1:T(8,128)(2,1)}, bf16[512,1024]{0,1:T(8,128)(2,1)S(1)}) fusion(bf16[1024,1024]{0,1:T(8,128)(2,1)} %get-tuple-element.512, s32[]{:T(128)S(6)} %select_n.96, bf16[1024,1024]{0,1:T(8,128)(2,1)} %get-tuple-element.510), kind=kLoop, calls=%fused_computation.20.clone.1 | loop fusion | bytes 4194308 | tf_op jit(solution)/shard_map/while/body/eval_jaxpr/dynamic_slice | solution.py:165
  96.3 4.7 %fusion.68 = (f32[128,8,4]{0,2,1:T(4,128)S(1)}, f32[8,512,128,4]{2,1,3,0:T(8,128)}) fusion(pred[128,512]{0,1:T(8,128)(4,1)S(1)} %broadcast_compare_fusion.2, bf16[512,8,128,1]{0,2,3,1:T(8,128)(2,1)S(1)} %bitcast.122, bf16[128,8,4,128]{3,0,2,1:T(8,128)(2,1)S(1)} %get-tuple-element.511), kind=kOutput, calls=%fused_computation.6.clone.1 | convolution fusion | flops 543158272 | bytes 10567680 | tf_op jit(solution)/shard_map/while/body/eval_jaxpr/qgkd,sgd->qgks/dot_general | solution.py:88
  101.0 4.8 %fusion.69 = f32[128,8,4]{0,2,1:T(4,128)S(1)} fusion(f32[8,512,128,4]{2,1,3,0:T(8,128)} %get-tuple-element.457, f32[128,8,4]{0,2,1:T(4,128)S(1)} %select_maximum_fusion.2, pred[128,512]{0,1:T(8,128)(4,1)S(1)} %broadcast_compare_fusion.2), kind=kLoop, calls=%fused_computation.8.clone.1 | loop fusion | flops 10481664 | bytes 8486912 | tf_op jit(solution)/shard_map/while/body/eval_jaxpr/reduce_sum | solution.py:97
  107.0 5.0 %bitcast_add_fusion.2 = f32[128,8,4,128]{0,3,2,1:T(8,128)} fusion(f32[128,8,4,128]{0,3,2,1:T(8,128)} %get-tuple-element.497, bf16[512,8,128,1]{0,2,3,1:T(8,128)(2,1)} %bitcast.124, f32[8,512,128,4]{2,1,3,0:T(8,128)S(1)} %copy-done, f32[128,8,4]{0,2,1:T(4,128)S(1)} %select_maximum_fusion.2, pred[128,512]{0,1:T(8,128)(4,1)S(1)} %broadcast_compare_fusion.2, ...), kind=kOutput, calls=%fused_computation.11.clone.1 | convolution fusion | flops 548929536 | bytes 13729793 | tf_op jit(solution)/shard_map/while/body/eval_jaxpr/qgks,sgd->qgkd/dot_general | solution.py:98
  112.0 1.9 %divide_convert_fusion = bf16[128,8,4,128]{0,3,2,1:T(8,128)(2,1)S(1)} fusion(f32[128,8,4,128]{0,3,2,1:T(8,128)} %get-tuple-element.261, f32[128,8,4]{0,2,1:T(4,128)S(1)} %get-tuple-element.262), kind=kLoop, calls=%fused_computation.40 | loop fusion | flops 1048576 | bytes 3162112 | tf_op jit(solution)/shard_map/convert_element_type | solution.py:181
  115.3 41.9 %all-gather.5.cloned.1.call-done = bf16[8,64,64,128]{3,2,1,0:T(8,128)(2,1)} async-done(((bf16[1,64,64,128]{3,2,1,0:T(8,128)(2,1)}), bf16[8,64,64,128]{3,2,1,0:T(8,128)(2,1)}) %all-gather.5.cloned.1.call-update) | async-done | bytes 8388624 | tf_op jit(solution)/shard_map/all_gather | solution.py:21
  157.2 19.8 %while.37 = (s32[]{:T(128)}, f32[64,64,128]{2,1,0:T(8,128)S(1)}, s32[]{:T(128)}, bf16[8,64]{1,0:T(8,128)(2,1)}, bf16[8,64,64,128]{3,2,1,0:T(8,128)(2,1)}, /*index=5*/s32[]{:T(128)}, s32[]{:T(128)}) while((s32[]{:T(128)}, f32[64,64,128]{2,1,0:T(8,128)S(1)}, s32[]{:T(128)}, bf16[8,64]{1,0:T(8,128)(2,1)}, ...), condition=%wide.region_2.3_spmd.clone, body=%wide.region_1.2_spmd.clone.sunk | while | flops 2621508 | bytes 5243625 | solution.py:38
  157.9 1.8 fusion.63
  160.4 1.8 fusion.63
  162.9 1.8 fusion.63
  177.0 4.3 %multiply_reduce_fusion = (f32[128,8,8]{0,2,1:T(8,128)S(1)}, f32[128,8,8,64]{0,3,2,1:T(8,128)S(1)}) fusion(bf16[128,4096]{0,1:T(8,128)(2,1)S(1)} %copy-done.1, f32[8,8,64,128]{3,2,1,0:T(8,128)S(1)} %bitcast.123, bf16[128,8,128,1]{2,1,0,3:T(8,128)(2,1)S(1)} %bitcast.128, f32[128,8,8]{0,2,1:T(8,128)S(1)} %get-tuple-element.365, ...), kind=kOutput, calls=%fused_computation.41 | convolution fusion | flops 811589632 | bytes 9764864 | tf_op jit(solution)/shard_map/tgn,gkpn->tgkp/dot_general | solution.py:185
  (77 shorter events, 30.1 us)
Async XLA Ops:
  7.2 5.3 %copy-start.2 = (bf16[128,4096]{1,0:T(8,128)(2,1)S(1)}, bf16[128,4096]{1,0:T(8,128)(2,1)}, u32[]{:S(2)}) copy-start(bf16[128,4096]{1,0:T(8,128)(2,1)} %param.14) | copy-start | bytes 3145732
  7.2 6.0 %copy-start.6 = (bf16[128,1024]{1,0:T(8,128)(2,1)S(1)}, bf16[128,1024]{1,0:T(8,128)(2,1)}, u32[]{:S(2)}) copy-start(bf16[128,1024]{1,0:T(8,128)(2,1)} %param.16) | copy-start | bytes 786436
  7.2 43.2 %all-gather.7.cloned.1.call-start = ((), (), s32[]{:S(2)}) async-start(), calls=%async_computation.1 | async-start | bytes 2359296 | tf_op jit(solution)/shard_map/all_gather | solution.py:158
  9.1 65.4 %all-gather.9.cloned.1.call-start = ((), (), s32[]{:S(2)}) async-start(), calls=%async_computation.2 | async-start | bytes 2359296 | tf_op jit(solution)/shard_map/all_gather | solution.py:159
  11.0 146.2 %all-gather.5.cloned.1.call-start = ((), (), s32[]{:S(2)}) async-start(), calls=%async_computation | async-start | bytes 9437184 | tf_op jit(solution)/shard_map/all_gather | solution.py:21
  13.1 2.5 %copy-start.4 = (bf16[128,4096]{0,1:T(8,128)(2,1)}, bf16[128,4096]{0,1:T(8,128)(2,1)S(1)}, u32[]{:S(2)}) copy-start(bf16[128,4096]{0,1:T(8,128)(2,1)S(1)} %copy.39) | copy-start | bytes 3145732
  13.1 2.5 %copy-start.8 = (u32[32]{0:T(128)S(1)}, u32[32]{0:T(128)}, u32[]{:S(2)}) copy-start(u32[32]{0:T(128)} %constant.120) | copy-start | bytes 388
  13.2 24.9 %copy-start.3 = (bf16[128,4096]{1,0:T(8,128)(2,1)S(1)}, bf16[128,4096]{1,0:T(8,128)(2,1)}, u32[]{:S(2)}) copy-start(bf16[128,4096]{1,0:T(8,128)(2,1)} %param.15) | copy-start | bytes 3145732
  43.4 3.8 %copy-start.5 = (bf16[128,4096]{0,1:T(8,128)(2,1)S(1)}, bf16[128,4096]{0,1:T(8,128)(2,1)}, u32[]{:S(2)}) copy-start(bf16[128,4096]{0,1:T(8,128)(2,1)} %copy-done.4) | copy-start | bytes 3145732
  82.0 6.9 %copy-start = (f32[8,512,128,4]{2,1,3,0:T(8,128)S(1)}, f32[8,512,128,4]{2,1,3,0:T(8,128)}, u32[]{:S(2)}) copy-start(f32[8,512,128,4]{2,1,3,0:T(8,128)} %get-tuple-element.457) | copy-start | bytes 25165828 | tf_op jit(solution)/shard_map/while
  101.0 6.0 %copy-start = (f32[8,512,128,4]{2,1,3,0:T(8,128)S(1)}, f32[8,512,128,4]{2,1,3,0:T(8,128)}, u32[]{:S(2)}) copy-start(f32[8,512,128,4]{2,1,3,0:T(8,128)} %get-tuple-element.457) | copy-start | bytes 25165828 | tf_op jit(solution)/shard_map/while
  157.2 19.8 %copy-start.1 = (bf16[128,4096]{0,1:T(8,128)(2,1)S(1)}, bf16[128,4096]{0,1:T(8,128)(2,1)}, u32[]{:S(2)}) copy-start(bf16[128,4096]{0,1:T(8,128)(2,1)} %copy.43) | copy-start | bytes 3145732
  177.0 4.3 %copy-start.7 = (f32[4096]{0:T(1024)S(1)}, f32[4096]{0:T(1024)}, u32[]{:S(2)}) copy-start(f32[4096]{0:T(1024)} %param.20) | copy-start | bytes 49156
Sparse Core Ops, SparseCore 0:
  9.6 33.5 all-gather.6
  44.8 29.6 all-gather.8
  76.1 81.0 all-gather.4
where the time goes:
time: 191 us; the launch traced here: 190 us
  waiting for transfers between devices  66.1 us (35%)
  other arithmetic  35 us (18%)
  matrix products  32.5 us (17%)
  local copies, waits for them, and re-layouts  22.5 us (12%)
  blocking collectives  19.1 us (10%)
  between operations  14.6 us (8%)
    all_gather x1, waiting for transfers between devices, entering(): lax.all_gather(part.astype(kind), axis)  41.9 us
    all_gather x1, waiting for transfers between devices, on_device(): value_piece = lax.all_gather(teacher_v, 'seq', axis=0, tiled=True)  24.1 us
    unnamed x1, blocking collectives  19.1 us
    select_n x8, other arithmetic, step(): return jax.tree.map(lambda a, b: jnp.where(reached, a, b), new, before)  14.1 us
    unnamed x28, local copies, waits for them, and re-layouts  12.8 us
    reduce_sum x2, other arithmetic, attend_block(): row_total = row_total * shrink + jnp.sum(probabilities, axis=3)  10.5 us
    dot_general x2, matrix products, attend_block(): jnp.einsum('qgks,sgd->qgkd', probabilities.astype(jnp.bfloat16), values_t...  9.59 us
    dot_general x2, matrix products, attend_block(): jnp.einsum('qgkd,sgd->qgks', query_four, keys_three, preferred_element_ty...  9.4 us
  transfers between devices with their start and end apart: 3, of which 2 were waited for; matrix products, arithmetic and copies ran while one was open for 31% of the time, Pallas kernels for 0%

commit v1 on v0

v1 whole, which is shorter than its diff:
```python
import functools
import math

import jax
import jax.numpy as jnp
from jax import lax
from jax.experimental import pallas as pl
from jax.experimental.pallas import tpu as pltpu
from jax.sharding import PartitionSpec as P

GROUPS = 8
HEAD_SIZE = 128
BLOCK = 128

epsilon_norm = 1e-05
masked_score = -1e30
F32 = jnp.float32
BF16 = jnp.bfloat16
MESH = pl.DeviceIdType.MESH


def dot(a, b, ca=1, cb=0):
    return lax.dot_general(a, b, (((ca,), (cb,)), ((), ())), preferred_element_type=F32)


def kernel(
    n,
    x_hbm, z_hbm, b_hbm, c_hbm, step_hbm, rate_ref, gain_ref, q_hbm, k_hbm, v_hbm,
    sout_hbm, tout_hbm,
    x_ref, z_ref, b_ref, c_ref, step_ref, q_ref, kbuf, vbuf,
    cum_ref, ssm_ref, stl_ref, stin_ref, stout_ref,
    qt_ref, acc_ref, max_ref, sum_ref, so_ref, to_ref,
    in_sem, k_send, k_recv, v_send, v_recv, s_send, s_recv, so_sem, to_sem,
):
    me = lax.axis_index("seq")
    right = lax.rem(me + 1, n)
    left = lax.rem(me + n - 1, n)
    has_left = me > 0
    has_right = me < n - 1
    tokens, width = x_ref.shape
    heads = step_ref.shape[0]
    per_group = heads // GROUPS
    head_width = width // heads
    gw = width // GROUPS
    state_dim = b_ref.shape[1] // GROUPS
    kv_count = k_hbm.shape[1] // HEAD_SIZE
    qw = q_ref.shape[1] // kv_count
    ratio = qw // HEAD_SIZE
    lanes = 128
    pack = lanes // head_width
    scale = math.log2(math.e) / math.sqrt(HEAD_SIZE)

    loads = [
        pltpu.make_async_copy(src, dst, in_sem.at[i])
        for i, (src, dst) in enumerate(
            (
                (step_hbm, step_ref), (q_hbm, q_ref), (k_hbm, kbuf.at[me]), (v_hbm, vbuf.at[me]),
                (b_hbm, b_ref), (c_hbm, c_ref), (x_hbm, x_ref), (z_hbm, z_ref),
            )
        )
    ]
    for load in loads:
        load.start()

    barrier = pltpu.get_barrier_semaphore()

    @pl.when(has_left)
    def _():
        pl.semaphore_signal(barrier, inc=1, device_id={"seq": left}, device_id_type=MESH)

    @pl.when(has_right)
    def _():
        pl.semaphore_signal(barrier, inc=1, device_id={"seq": right}, device_id_type=MESH)

    pl.semaphore_wait(barrier, has_left.astype(jnp.int32) + has_right.astype(jnp.int32))

    def kv_copy(slot, k_src, v_src):
        return (
            pltpu.make_async_remote_copy(
                src_ref=k_src, dst_ref=kbuf.at[slot], send_sem=k_send.at[slot],
                recv_sem=k_recv.at[slot], device_id={"seq": right}, device_id_type=MESH,
            ),
            pltpu.make_async_remote_copy(
                src_ref=v_src, dst_ref=vbuf.at[slot], send_sem=v_send.at[slot],
                recv_sem=v_recv.at[slot], device_id={"seq": right}, device_id_type=MESH,
            ),
        )

    def state_copy(g):
        return pltpu.make_async_remote_copy(
            src_ref=stout_ref.at[g], dst_ref=stin_ref.at[g], send_sem=s_send.at[g],
            recv_sem=s_recv.at[g], device_id={"seq": right}, device_id_type=MESH,
        )

    @pl.when(has_right)
    def _():
        for copy in kv_copy(me, k_hbm, v_hbm):
            copy.start()

    def span(g, size):
        return pl.ds(pl.multiple_of(g * size, 128), size)

    loads[0].wait()
    eye = lax.broadcasted_iota(jnp.int32, (heads, heads), 0) == lax.broadcasted_iota(
        jnp.int32, (heads, heads), 1
    )
    rate = jnp.sum(jnp.where(eye, rate_ref[...], 0.0), axis=1, keepdims=True)
    running = -step_ref[...] * rate
    position = lax.broadcasted_iota(jnp.int32, (heads, tokens), 1)
    shift = 1
    while shift < tokens:
        running = running + jnp.where(position >= shift, pltpu.roll(running, shift, 1), 0.0)
        shift *= 2
    cum_ref[...] = running

    loads[1].wait()
    loads[2].wait()
    loads[3].wait()
    key_at = lax.broadcasted_iota(jnp.int32, (tokens, tokens), 0)
    query_at = lax.broadcasted_iota(jnp.int32, (tokens, tokens), 1)
    visible = jnp.concatenate([(key_at <= query_at).astype(F32)] * ratio, axis=1) > 0.5

    @pl.loop(0, kv_count)
    def _(g):
        for h in range(ratio):
            piece = q_ref[:, pl.ds(pl.multiple_of(g * qw + h * HEAD_SIZE, 128), HEAD_SIZE)]
            qt_ref[g, :, h * HEAD_SIZE : (h + 1) * HEAD_SIZE] = piece.T
        scores = dot(kbuf[me, :, span(g, HEAD_SIZE)], qt_ref[g]) * scale
        scores = jnp.where(visible, scores, masked_score)
        top = jnp.max(scores, axis=0, keepdims=True)
        weight = jnp.exp2(scores - top)
        max_ref[g] = top
        sum_ref[g] = jnp.sum(weight, axis=0, keepdims=True)
        acc_ref[g] = dot(vbuf[me, :, span(g, HEAD_SIZE)], weight.astype(BF16), 0, 0)

    for load in loads[4:]:
        load.wait()

    lower = query_at <= key_at
    low_half = lax.broadcasted_iota(jnp.int32, (tokens, lanes), 1) // head_width

    def spread(columns, p):
        out = columns[:, p * pack : p * pack + 1]
        for j in range(1, pack):
            at = p * pack + j
            out = jnp.where(low_half == j, columns[:, at : at + 1], out)
        return jnp.broadcast_to(out, (columns.shape[0], lanes))

    def student_local(g):
        cum = cum_ref[pl.ds(pl.multiple_of(g * per_group, 8), per_group), :]
        cum_t = cum.T
        tail_t = jnp.exp(cum[:, tokens - 1 : tokens] - cum).T
        b = b_ref[:, span(g, state_dim)]
        c = c_ref[:, span(g, state_dim)]
        products = dot(c, b, 1, 1)
        scaled = []
        for p in range(per_group // pack):
            x = x_ref[:, pl.ds(pl.multiple_of(g * gw + p * lanes, 128), lanes)].astype(F32)
            mixes = []
            sources = []
            for j in range(pack):
                h = p * pack + j
                difference = jnp.where(lower, cum_t[:, h : h + 1] - cum[h : h + 1, :], masked_score)
                mixes.append((products * jnp.exp(difference)).astype(BF16))
                sources.append(jnp.where(low_half == j, x, 0.0).astype(BF16))
            ssm_ref[g, :, p * lanes : (p + 1) * lanes] = dot(
                jnp.concatenate(mixes, axis=1), jnp.concatenate(sources, axis=0)
            )
            scaled.append((x * spread(tail_t, p)).astype(BF16))
        stl_ref[g] = dot(b, jnp.concatenate(scaled, axis=1), 0, 0)

    def attend(slot):
        @pl.loop(0, kv_count)
        def _(g):
            scores = dot(kbuf[slot, :, span(g, HEAD_SIZE)], qt_ref[g]) * scale
            old = max_ref[g]
            top = jnp.maximum(old, jnp.max(scores, axis=0, keepdims=True))
            shrink = jnp.exp2(old - top)
            weight = jnp.exp2(scores - top)
            max_ref[g] = top
            sum_ref[g] = sum_ref[g] * shrink + jnp.sum(weight, axis=0, keepdims=True)
            acc_ref[g] = acc_ref[g] * shrink + dot(
                vbuf[slot, :, span(g, HEAD_SIZE)], weight.astype(BF16), 0, 0
            )

    @pl.loop(0, max(n, GROUPS))
    def _(r):
        @pl.when(r < GROUPS)
        def _():
            student_local(r)

        @pl.when(r < me)
        def _():
            slot = me - 1 - r
            k_copy, v_copy = kv_copy(slot, kbuf.at[slot], vbuf.at[slot])
            k_copy.wait_recv()

            @pl.when(has_right)
            def _():
                k_copy.start()

            v_copy.wait_recv()

            @pl.when(has_right)
            def _():
                v_copy.start()

            attend(slot)

    @pl.loop(0, kv_count)
    def _(g):
        result = acc_ref[g] / sum_ref[g]
        for h in range(ratio):
            to_ref[:, pl.ds(pl.multiple_of(g * qw + h * HEAD_SIZE, 128), HEAD_SIZE)] = (
                result[:, h * HEAD_SIZE : (h + 1) * HEAD_SIZE].T.astype(BF16)
            )

    t_copy = pltpu.make_async_copy(to_ref, tout_hbm, to_sem)
    t_copy.start()

    @pl.when(me == 0)
    def _():
        stin_ref[...] = jnp.zeros_like(stin_ref)

    mean_of = jnp.where(
        lax.broadcasted_iota(jnp.int32, (lanes, lanes), 0) // head_width
        == lax.broadcasted_iota(jnp.int32, (lanes, lanes), 1) // head_width,
        1.0 / head_width,
        0.0,
    ).astype(BF16)
    row_half = lax.broadcasted_iota(jnp.int32, (1, lanes), 1) // head_width

    def out_copy(g):
        return pltpu.make_async_copy(
            so_ref.at[g], sout_hbm.at[:, span(g, gw)], so_sem.at[g]
        )

    @pl.loop(0, GROUPS)
    def _(g):
        cum = cum_ref[pl.ds(pl.multiple_of(g * per_group, 8), per_group), :]
        total = jnp.exp(cum[:, tokens - 1 : tokens])
        reach_t = jnp.exp(cum).T
        c = c_ref[:, span(g, state_dim)]

        @pl.when(has_left)
        def _():
            state_copy(g).wait_recv()

        state = stin_ref[g]

        @pl.when(has_right)
        def _():
            for p in range(per_group // pack):
                at = slice(p * lanes, (p + 1) * lanes)
                decay = total[p * pack : p * pack + 1, :]
                for j in range(1, pack):
                    decay = jnp.where(row_half == j, total[p * pack + j : p * pack + j + 1, :], decay)
                stout_ref[g, :, at] = (
                    state[:, at].astype(F32) * decay + stl_ref[g, :, at]
                ).astype(BF16)
            state_copy(g).start()

        carried = dot(c, state)
        for p in range(per_group // pack):
            at = slice(p * lanes, (p + 1) * lanes)
            cols = pl.ds(pl.multiple_of(g * gw + p * lanes, 128), lanes)
            ssm = ssm_ref[g, :, at] + carried[:, at] * spread(reach_t, p)
            z = z_ref[:, cols].astype(F32)
            gated = ssm * (z / (1.0 + jnp.exp(-z)))
            square = gated * gated
            high = square.astype(BF16)
            low = (square - high.astype(F32)).astype(BF16)
            mean = dot(high, mean_of) + dot(low, mean_of)
            so_ref[g, :, at] = (
                gated * lax.rsqrt(mean + epsilon_norm) * gain_ref[:, cols]
            ).astype(BF16)
        out_copy(g).start()

    t_copy.wait()

    @pl.loop(0, GROUPS)
    def _(g):
        out_copy(g).wait()

        @pl.when(has_right)
        def _():
            state_copy(g).wait_send()

    @pl.when(has_right)
    def _():
        for copy in kv_copy(me, k_hbm, v_hbm):
            copy.wait_send()

        @pl.loop(0, me)
        def _(slot):
            for copy in kv_copy(slot, kbuf.at[slot], vbuf.at[slot]):
                copy.wait_send()


def on_device(
    student_x, student_z, student_b, student_c, step_size, decay_rate, norm_gain,
    teacher_q, teacher_k, teacher_v,
):
    n = lax.axis_size("seq")
    tokens, width = student_x.shape
    heads = step_size.shape[0]
    assert tokens == BLOCK
    gw = width // GROUPS
    state_dim = student_b.shape[1] // GROUPS
    kv_count = teacher_k.shape[1] // HEAD_SIZE
    qw = teacher_q.shape[1] // kv_count
    hbm = pl.BlockSpec(memory_space=pl.ANY)
    vmem = pl.BlockSpec(memory_space=pltpu.VMEM)
    dma = pltpu.SemaphoreType.DMA
    return pl.pallas_call(
        functools.partial(kernel, n),
        out_shape=(
            jax.ShapeDtypeStruct(student_x.shape, BF16),
            jax.ShapeDtypeStruct(teacher_q.shape, BF16),
        ),
        in_specs=[hbm, hbm, hbm, hbm, hbm, vmem, vmem, hbm, hbm, hbm],
        out_specs=(hbm, hbm),
        scratch_shapes=[
            pltpu.VMEM(student_x.shape, BF16),
            pltpu.VMEM(student_z.shape, BF16),
            pltpu.VMEM(student_b.shape, BF16),
            pltpu.VMEM(student_c.shape, BF16),
            pltpu.VMEM(step_size.shape, F32),
            pltpu.VMEM(teacher_q.shape, BF16),
            pltpu.VMEM((n,) + teacher_k.shape, BF16),
            pltpu.VMEM((n,) + teacher_v.shape, BF16),
            pltpu.VMEM(step_size.shape, F32),
            pltpu.VMEM((GROUPS, tokens, gw), F32),
            pltpu.VMEM((GROUPS, state_dim, gw), F32),
            pltpu.VMEM((GROUPS, state_dim, gw), BF16),
            pltpu.VMEM((GROUPS, state_dim, gw), BF16),
            pltpu.VMEM((kv_count, HEAD_SIZE, qw), BF16),
            pltpu.VMEM((kv_count, HEAD_SIZE, qw), F32),
            pltpu.VMEM((kv_count, 1, qw), F32),
            pltpu.VMEM((kv_count, 1, qw), F32),
            pltpu.VMEM((GROUPS, tokens, gw), BF16),
            pltpu.VMEM(teacher_q.shape, BF16),
            dma((8,)),
            dma((n,)),
            dma((n,)),
            dma((n,)),
            dma((n,)),
            dma((GROUPS,)),
            dma((GROUPS,)),
            dma((GROUPS,)),
            dma,
        ],
        compiler_params=pltpu.CompilerParams(
            collective_id=0, has_side_effects=True, vmem_limit_bytes=56 * 1024 * 1024
        ),
    )(
        student_x, student_z, student_b, student_c, step_size, decay_rate[None, :],
        norm_gain[None, :], teacher_q, teacher_k, teacher_v,
    )


def solution(mesh):
    return jax.shard_map(
        on_device,
        mesh=mesh,
        in_specs=(
            P(("dp", "seq"), None),
            P(("dp", "seq"), None),
            P(("dp", "seq"), None),
            P(("dp", "seq"), None),
            P(None, ("dp", "seq")),
            P(),
            P(),
            P(("dp", "seq"), None),
            P(("dp", "seq"), None),
            P(("dp", "seq"), None),
        ),
        out_specs=(P(("dp", "seq"), None), P(("dp", "seq"), None)),
        check_vma=False,
    )
```

time: 191 us -> 56.5 us (0.30)
  the two profiles are of different devices: /device:TPU:0 before, /device:TPU:31 now
where the time goes in v1:
time: 56.5 us; the launch traced here: 56.3 us
  Pallas kernels  52.3 us (93%)
  local copies, waits for them, and re-layouts  3.35 us (6%)
  between operations  0.65 us (1%)
    pallas_call x1, Pallas kernels, on_device(): pl.pallas_call(functools.partial(kernel, n), out_shape=(jax.ShapeDtypeStr...  52.3 us
    unnamed x4, local copies, waits for them, and re-layouts  3.35 us

profile of v1, /device:TPU:31, one launch (start us, length us, event | category | flops | bytes accessed | tf_op | source)
XLA Modules:
  0.0 56.3 jit_solution(2148982023164603349)
XLA Ops:
  0.6 52.3 %shard_map.113 = (bf16[128,4096]{1,0:T(8,128)(2,1)}, bf16[128,4096]{1,0:T(8,128)(2,1)}) custom-call(bf16[128,4096]{1,0:T(8,128)(2,1)} %x_hbm.1, bf16[128,4096]{1,0:T(8,128)(2,1)} %z_hbm.1, bf16[128,1024]{1,0:T(8,128)(2,1)} %b_hbm.1, bf16[128,1024]{1,0:T(8,128)(2,1)} %c_hbm.1, f32[64,128]{1,0:T(8,128)} %step_hbm.1, f32[1,64]{1,0:T(1,128)} %bitcast.3, ...), custom_call_target="tpu_custom_call" | custom-call | tf_op jit(solution)/shard_map/pallas_call | solution.py:315
  52.9 0.0 copy-start
  52.9 2.4 %copy.14 = bf16[128,4096]{1,0:T(8,128)(2,1)} copy(bf16[128,4096]{1,0:T(8,128)(2,1)} %get-tuple-element.4) | data formatting | bytes 2097152
  55.3 0.0 copy-done
  55.3 1.0 %copy.15 = bf16[128,4096]{1,0:T(8,128)(2,1)} copy(bf16[128,4096]{1,0:T(8,128)(2,1)S(1)} %copy-done) | data formatting | bytes 2097152
Async XLA Ops:
  52.9 2.4 %copy-start = (bf16[128,4096]{1,0:T(8,128)(2,1)S(1)}, bf16[128,4096]{1,0:T(8,128)(2,1)}, u32[]{:S(2)}) copy-start(bf16[128,4096]{1,0:T(8,128)(2,1)} %get-tuple-element.5) | copy-start | bytes 3145732

commit v2 on v1

--- a/solution.py
+++ b/solution.py
@@ -11,6 +11,7 @@
 GROUPS = 8
 HEAD_SIZE = 128
 BLOCK = 128
+CUTS = 2
 
 epsilon_norm = 1e-05
 masked_score = -1e30
@@ -26,11 +27,11 @@
 def kernel(
     n,
     x_hbm, z_hbm, b_hbm, c_hbm, step_hbm, rate_ref, gain_ref, q_hbm, k_hbm, v_hbm,
-    sout_hbm, tout_hbm,
+    so_ref, to_ref,
     x_ref, z_ref, b_ref, c_ref, step_ref, q_ref, kbuf, vbuf,
-    cum_ref, ssm_ref, stl_ref, stin_ref, stout_ref,
-    qt_ref, acc_ref, max_ref, sum_ref, so_ref, to_ref,
-    in_sem, k_send, k_recv, v_send, v_recv, s_send, s_recv, so_sem, to_sem,
+    cum_ref, ssm_ref, reach_ref, stl_ref, stin_ref, stout_ref,
+    qt_ref, acc_ref, max_ref, sum_ref,
+    in_sem, k_send, k_recv, v_send, v_recv, s_send, s_recv,
 ):
     me = lax.axis_index("seq")
     right = lax.rem(me + 1, n)
@@ -86,10 +87,10 @@
             ),
         )
 
-    def state_copy(g):
+    def state_copy(g, cut):
         return pltpu.make_async_remote_copy(
-            src_ref=stout_ref.at[g], dst_ref=stin_ref.at[g], send_sem=s_send.at[g],
-            recv_sem=s_recv.at[g], device_id={"seq": right}, device_id_type=MESH,
+            src_ref=stout_ref.at[g, cut], dst_ref=stin_ref.at[g, cut], send_sem=s_send.at[g, cut],
+            recv_sem=s_recv.at[g, cut], device_id={"seq": right}, device_id_type=MESH,
         )
 
     @pl.when(has_right)
@@ -113,11 +114,73 @@
         shift *= 2
     cum_ref[...] = running
 
-    loads[1].wait()
-    loads[2].wait()
-    loads[3].wait()
     key_at = lax.broadcasted_iota(jnp.int32, (tokens, tokens), 0)
     query_at = lax.broadcasted_iota(jnp.int32, (tokens, tokens), 1)
+    half = lax.broadcasted_iota(jnp.int32, (tokens, lanes), 1) // head_width
+    row_half = lax.broadcasted_iota(jnp.int32, (1, lanes), 1) // head_width
+    pairs = per_group // pack
+    cut_pairs = pairs // CUTS
+
+    def spread(columns, p):
+        out = columns[:, p * pack : p * pack + 1]
+        for j in range(1, pack):
+            at = p * pack + j
+            out = jnp.where(half == j, columns[:, at : at + 1], out)
+        return jnp.broadcast_to(out, (columns.shape[0], lanes))
+
+    def columns_of(g, p):
+        return pl.ds(pl.multiple_of(g * gw + p * lanes, 128), lanes)
+
+    loads[4].wait()
+    loads[6].wait()
+
+    @pl.loop(0, GROUPS)
+    def _(g):
+        cum = cum_ref[pl.ds(pl.multiple_of(g * per_group, 8), per_group), :]
+        tail_t = jnp.exp(cum[:, tokens - 1 : tokens] - cum).T
+        scaled = [
+            (x_ref[:, columns_of(g, p)].astype(F32) * spread(tail_t, p)).astype(BF16)
+            for p in range(pairs)
+        ]
+        added = dot(b_ref[:, span(g, state_dim)], jnp.concatenate(scaled, axis=1), 0, 0)
+        stl_ref[g] = added
+
+        @pl.when(me == 0)
+        def _():
+            for cut in range(CUTS):
+                size = gw // CUTS
+                stout_ref[g, cut] = added[:, cut * size : (cut + 1) * size].astype(BF16)
+                stin_ref[g, cut] = jnp.zeros((state_dim, size), BF16)
+
+    @pl.when(jnp.logical_and(me == 0, has_right))
+    def _():
+        @pl.loop(0, GROUPS)
+        def _(g):
+            for cut in range(CUTS):
+                state_copy(g, cut).start()
+
+    def relay(slot):
+        k_copy, v_copy = kv_copy(slot, kbuf.at[slot], vbuf.at[slot])
+        k_copy.wait_recv()
+
+        @pl.when(has_right)
+        def _():
+            k_copy.start()
+
+        v_copy.wait_recv()
+
+        @pl.when(has_right)
+        def _():
+            v_copy.start()
+
+    near = lax.rem(me, 2) == 1
+
+    @pl.when(near)
+    def _():
+        relay(me - 1)
+
+    for i in (1, 2, 3):
+        loads[i].wait()
     visible = jnp.concatenate([(key_at <= query_at).astype(F32)] * ratio, axis=1) > 0.5
 
     @pl.loop(0, kv_count)
@@ -133,41 +196,31 @@
         sum_ref[g] = jnp.sum(weight, axis=0, keepdims=True)
         acc_ref[g] = dot(vbuf[me, :, span(g, HEAD_SIZE)], weight.astype(BF16), 0, 0)
 
-    for load in loads[4:]:
-        load.wait()
-
+    loads[5].wait()
+    loads[7].wait()
     lower = query_at <= key_at
-    low_half = lax.broadcasted_iota(jnp.int32, (tokens, lanes), 1) // head_width
-
-    def spread(columns, p):
-        out = columns[:, p * pack : p * pack + 1]
-        for j in range(1, pack):
-            at = p * pack + j
-            out = jnp.where(low_half == j, columns[:, at : at + 1], out)
-        return jnp.broadcast_to(out, (columns.shape[0], lanes))
 
     def student_local(g):
         cum = cum_ref[pl.ds(pl.multiple_of(g * per_group, 8), per_group), :]
         cum_t = cum.T
-        tail_t = jnp.exp(cum[:, tokens - 1 : tokens] - cum).T
-        b = b_ref[:, span(g, state_dim)]
-        c = c_ref[:, span(g, state_dim)]
-        products = dot(c, b, 1, 1)
-        scaled = []
-        for p in range(per_group // pack):
-            x = x_ref[:, pl.ds(pl.multiple_of(g * gw + p * lanes, 128), lanes)].astype(F32)
+        reach_t = jnp.exp(cum).T
+        products = dot(c_ref[:, span(g, state_dim)], b_ref[:, span(g, state_dim)], 1, 1)
+        for p in range(pairs):
+            x = x_ref[:, columns_of(g, p)].astype(F32)
             mixes = []
             sources = []
             for j in range(pack):
                 h = p * pack + j
                 difference = jnp.where(lower, cum_t[:, h : h + 1] - cum[h : h + 1, :], masked_score)
                 mixes.append((products * jnp.exp(difference)).astype(BF16))
-                sources.append(jnp.where(low_half == j, x, 0.0).astype(BF16))
-            ssm_ref[g, :, p * lanes : (p + 1) * lanes] = dot(
+                sources.append(jnp.where(half == j, x, 0.0).astype(BF16))
+            z = z_ref[:, columns_of(g, p)].astype(F32)
+            gate = z / (1.0 + jnp.exp(-z))
+            at = slice(p * lanes, (p + 1) * lanes)
+            ssm_ref[g, :, at] = gate * dot(
                 jnp.concatenate(mixes, axis=1), jnp.concatenate(sources, axis=0)
             )
-            scaled.append((x * spread(tail_t, p)).astype(BF16))
-        stl_ref[g] = dot(b, jnp.concatenate(scaled, axis=1), 0, 0)
+            reach_ref[g, :, at] = gate * spread(reach_t, p)
 
     def attend(slot):
         @pl.loop(0, kv_count)
@@ -191,21 +244,11 @@
 
         @pl.when(r < me)
         def _():
-            slot = me - 1 - r
-            k_copy, v_copy = kv_copy(slot, kbuf.at[slot], vbuf.at[slot])
-            k_copy.wait_recv()
-
-            @pl.when(has_right)
+            @pl.when(jnp.logical_or(r > 0, jnp.logical_not(near)))
             def _():
-                k_copy.start()
-
-            v_copy.wait_recv()
-
-            @pl.when(has_right)
-            def _():
-                v_copy.start()
-
-            attend(slot)
+                relay(me - 1 - r)
+
+            attend(me - 1 - r)
 
     @pl.loop(0, kv_count)
     def _(g):
@@ -215,79 +258,59 @@
                 result[:, h * HEAD_SIZE : (h + 1) * HEAD_SIZE].T.astype(BF16)
             )
 
-    t_copy = pltpu.make_async_copy(to_ref, tout_hbm, to_sem)
-    t_copy.start()
-
-    @pl.when(me == 0)
-    def _():
-        stin_ref[...] = jnp.zeros_like(stin_ref)
-
     mean_of = jnp.where(
         lax.broadcasted_iota(jnp.int32, (lanes, lanes), 0) // head_width
         == lax.broadcasted_iota(jnp.int32, (lanes, lanes), 1) // head_width,
         1.0 / head_width,
         0.0,
     ).astype(BF16)
-    row_half = lax.broadcasted_iota(jnp.int32, (1, lanes), 1) // head_width
-
-    def out_copy(g):
-        return pltpu.make_async_copy(
-            so_ref.at[g], sout_hbm.at[:, span(g, gw)], so_sem.at[g]
-        )
 
     @pl.loop(0, GROUPS)
     def _(g):
         cum = cum_ref[pl.ds(pl.multiple_of(g * per_group, 8), per_group), :]
         total = jnp.exp(cum[:, tokens - 1 : tokens])
-        reach_t = jnp.exp(cum).T
         c = c_ref[:, span(g, state_dim)]
-
-        @pl.when(has_left)
-        def _():
-            state_copy(g).wait_recv()
-
-        state = stin_ref[g]
-
-        @pl.when(has_right)
-        def _():
-            for p in range(per_group // pack):
+        for cut in range(CUTS):
+
+            @pl.when(has_left)
+            def _():
+                state_copy(g, cut).wait_recv()
+
+            state = stin_ref[g, cut]
+
+            @pl.when(jnp.logical_and(has_left, has_right))
+            def _():
+                for i in range(cut_pairs):
+                    p = cut * cut_pairs + i
+                    at = slice(i * lanes, (i + 1) * lanes)
+                    decay = total[p * pack : p * pack + 1, :]
+                    for j in range(1, pack):
+                        decay = jnp.where(
+                            row_half == j, total[p * pack + j : p * pack + j + 1, :], decay
+                        )
+                    stout_ref[g, cut, :, at] = (
+                        state[:, at].astype(F32) * decay
+                        + stl_ref[g, :, p * lanes : (p + 1) * lanes]
+                    ).astype(BF16)
+                state_copy(g, cut).start()
+
+            carried = dot(c, state)
+            for i in range(cut_pairs):
+                p = cut * cut_pairs + i
                 at = slice(p * lanes, (p + 1) * lanes)
-                decay = total[p * pack : p * pack + 1, :]
-                for j in range(1, pack):
-                    decay = jnp.where(row_half == j, total[p * pack + j : p * pack + j + 1, :], decay)
-                stout_ref[g, :, at] = (
-                    state[:, at].astype(F32) * decay + stl_ref[g, :, at]
+                gated = ssm_ref[g, :, at] + reach_ref[g, :, at] * carried[:, i * lanes : (i + 1) * lanes]
+                mean = dot((gated * gated).astype(BF16), mean_of)
+                so_ref[:, columns_of(g, p)] = (
+                    gated * lax.rsqrt(mean + epsilon_norm) * gain_ref[:, columns_of(g, p)]
                 ).astype(BF16)
-            state_copy(g).start()
-
-        carried = dot(c, state)
-        for p in range(per_group // pack):
-            at = slice(p * lanes, (p + 1) * lanes)
-            cols = pl.ds(pl.multiple_of(g * gw + p * lanes, 128), lanes)
-            ssm = ssm_ref[g, :, at] + carried[:, at] * spread(reach_t, p)
-            z = z_ref[:, cols].astype(F32)
-            gated = ssm * (z / (1.0 + jnp.exp(-z)))
-            square = gated * gated
-            high = square.astype(BF16)
-            low = (square - high.astype(F32)).astype(BF16)
-            mean = dot(high, mean_of) + dot(low, mean_of)
-            so_ref[g, :, at] = (
-                gated * lax.rsqrt(mean + epsilon_norm) * gain_ref[:, cols]
-            ).astype(BF16)
-        out_copy(g).start()
-
-    t_copy.wait()
-
-    @pl.loop(0, GROUPS)
-    def _(g):
-        out_copy(g).wait()
-
-        @pl.when(has_right)
-        def _():
-            state_copy(g).wait_send()
 
     @pl.when(has_right)
     def _():
+        @pl.loop(0, GROUPS)
+        def _(g):
+            for cut in range(CUTS):
+                state_copy(g, cut).wait_send()
+
         for copy in kv_copy(me, k_hbm, v_hbm):
             copy.wait_send()
 
@@ -295,6 +318,17 @@
         def _(slot):
             for copy in kv_copy(slot, kbuf.at[slot], vbuf.at[slot]):
                 copy.wait_send()
+
+
+def store(s_ref, t_ref, s_out, t_out, sem):
+    copies = [
+        pltpu.make_async_copy(s_ref, s_out, sem.at[0]),
+        pltpu.make_async_copy(t_ref, t_out, sem.at[1]),
+    ]
+    for copy in copies:
+        copy.start()
+    for copy in copies:
+        copy.wait()
 
 
 def on_device(
@@ -312,14 +346,14 @@
     hbm = pl.BlockSpec(memory_space=pl.ANY)
     vmem = pl.BlockSpec(memory_space=pltpu.VMEM)
     dma = pltpu.SemaphoreType.DMA
-    return pl.pallas_call(
+    results = pl.pallas_call(
         functools.partial(kernel, n),
         out_shape=(
-            jax.ShapeDtypeStruct(student_x.shape, BF16),
-            jax.ShapeDtypeStruct(teacher_q.shape, BF16),
+            pltpu.VMEM(student_x.shape, BF16),
+            pltpu.VMEM(teacher_q.shape, BF16),
         ),
         in_specs=[hbm, hbm, hbm, hbm, hbm, vmem, vmem, hbm, hbm, hbm],
-        out_specs=(hbm, hbm),
+        out_specs=(vmem, vmem),
         scratch_shapes=[
             pltpu.VMEM(student_x.shape, BF16),
             pltpu.VMEM(student_z.shape, BF16),
@@ -331,24 +365,21 @@
             pltpu.VMEM((n,) + teacher_v.shape, BF16),
             pltpu.VMEM(step_size.shape, F32),
             pltpu.VMEM((GROUPS, tokens, gw), F32),
+            pltpu.VMEM((GROUPS, tokens, gw), F32),
             pltpu.VMEM((GROUPS, state_dim, gw), F32),
-            pltpu.VMEM((GROUPS, state_dim, gw), BF16),
-            pltpu.VMEM((GROUPS, state_dim, gw), BF16),
+            pltpu.VMEM((GROUPS, CUTS, state_dim, gw // CUTS), BF16),
+            pltpu.VMEM((GROUPS, CUTS, state_dim, gw // CUTS), BF16),
             pltpu.VMEM((kv_count, HEAD_SIZE, qw), BF16),
             pltpu.VMEM((kv_count, HEAD_SIZE, qw), F32),
             pltpu.VMEM((kv_count, 1, qw), F32),
             pltpu.VMEM((kv_count, 1, qw), F32),
-            pltpu.VMEM((GROUPS, tokens, gw), BF16),
-            pltpu.VMEM(teacher_q.shape, BF16),
             dma((8,)),
             dma((n,)),
             dma((n,)),
             dma((n,)),
             dma((n,)),
-            dma((GROUPS,)),
-            dma((GROUPS,)),
-            dma((GROUPS,)),
-            dma,
+            dma((GROUPS, CUTS)),
+            dma((GROUPS, CUTS)),
         ],
         compiler_params=pltpu.CompilerParams(
             collective_id=0, has_side_effects=True, vmem_limit_bytes=56 * 1024 * 1024
@@ -357,6 +388,17 @@
         student_x, student_z, student_b, student_c, step_size, decay_rate[None, :],
         norm_gain[None, :], teacher_q, teacher_k, teacher_v,
     )
+    results = [pltpu.with_memory_space_constraint(r, pltpu.VMEM) for r in results]
+    return pl.pallas_call(
+        store,
+        out_shape=(
+            jax.ShapeDtypeStruct(student_x.shape, BF16),
+            jax.ShapeDtypeStruct(teacher_q.shape, BF16),
+        ),
+        in_specs=[vmem, vmem],
+        out_specs=(hbm, hbm),
+        scratch_shapes=[dma((2,))],
+    )(*results)
 
 
 def solution(mesh):

time: 56.5 us -> 56.1 us (level)
  local copies, waits for them, and re-layouts: 3.35 us -> 0 us
  Pallas kernels: 52.3 us -> 55.2 us
    unnamed x4 -> x0, local copies, waits for them, and re-layouts: 3.35 us -> none
    pallas_call x1 -> x2, Pallas kernels: 52.3 us -> 55.2 us  [the longest x1 53.9 us: on_device(): pl.pallas_call(functools.partial(kernel, n), out_shape=(pltpu.VMEM(studen...]
where the time goes in v2:
time: 56.1 us; the launch traced here: 55.9 us
  Pallas kernels  55.2 us (98%)
  between operations  0.64 us (1%)
    pallas_call x1, Pallas kernels, on_device(): pl.pallas_call(functools.partial(kernel, n), out_shape=(pltpu.VMEM(studen...  53.9 us
    pallas_call x1, Pallas kernels, on_device(): pl.pallas_call(store, out_shape=(jax.ShapeDtypeStruct(student_x.shape, BF...  1.33 us

profile of v2, /device:TPU:31, one launch (start us, length us, event | category | flops | bytes accessed | tf_op | source)
XLA Modules:
  0.0 55.9 jit_solution(4878019048863778594)
XLA Ops:
  0.6 53.9 %shard_map.113 = (bf16[128,4096]{1,0:T(8,128)(2,1)S(1)}, bf16[128,4096]{1,0:T(8,128)(2,1)S(1)}) custom-call(bf16[128,4096]{1,0:T(8,128)(2,1)} %x_hbm.1, bf16[128,4096]{1,0:T(8,128)(2,1)} %z_hbm.1, bf16[128,1024]{1,0:T(8,128)(2,1)} %b_hbm.1, bf16[128,1024]{1,0:T(8,128)(2,1)} %c_hbm.1, f32[64,128]{1,0:T(8,128)} %step_hbm.1, f32[1,64]{1,0:T(1,128)} %bitcast.3, ...), custom_call_target="tpu_custom_call" | custom-call | tf_op jit(solution)/shard_map/pallas_call | solution.py:349
  54.5 1.3 %shard_map.114 = (bf16[128,4096]{1,0:T(8,128)(2,1)}, bf16[128,4096]{1,0:T(8,128)(2,1)}) custom-call(bf16[128,4096]{1,0:T(8,128)(2,1)S(1)} %get-tuple-element.4.s_ref, bf16[128,4096]{1,0:T(8,128)(2,1)S(1)} %get-tuple-element.5.t_ref), custom_call_target="tpu_custom_call" | custom-call | tf_op jit(solution)/shard_map/pallas_call | solution.py:392

commit v3 on v2

--- a/solution.py
+++ b/solution.py
@@ -75,16 +75,16 @@
 
     pl.semaphore_wait(barrier, has_left.astype(jnp.int32) + has_right.astype(jnp.int32))
 
-    def kv_copy(slot, k_src, v_src):
-        return (
-            pltpu.make_async_remote_copy(
-                src_ref=k_src, dst_ref=kbuf.at[slot], send_sem=k_send.at[slot],
-                recv_sem=k_recv.at[slot], device_id={"seq": right}, device_id_type=MESH,
-            ),
-            pltpu.make_async_remote_copy(
-                src_ref=v_src, dst_ref=vbuf.at[slot], send_sem=v_send.at[slot],
-                recv_sem=v_recv.at[slot], device_id={"seq": right}, device_id_type=MESH,
-            ),
+    def key_copy(slot, source):
+        return pltpu.make_async_remote_copy(
+            src_ref=source, dst_ref=kbuf.at[slot], send_sem=k_send.at[slot],
+            recv_sem=k_recv.at[slot], device_id={"seq": right}, device_id_type=MESH,
+        )
+
+    def value_copy(slot, source):
+        return pltpu.make_async_remote_copy(
+            src_ref=source, dst_ref=vbuf.at[slot], send_sem=v_send.at[slot],
+            recv_sem=v_recv.at[slot], device_id={"seq": right}, device_id_type=MESH,
         )
 
     def state_copy(g, cut):
@@ -95,7 +95,7 @@
 
     @pl.when(has_right)
     def _():
-        for copy in kv_copy(me, k_hbm, v_hbm):
+        for copy in (key_copy(me, k_hbm), value_copy(me, v_hbm)):
             copy.start()
 
     def span(g, size):
@@ -121,70 +121,28 @@
     pairs = per_group // pack
     cut_pairs = pairs // CUTS
 
-    def spread(columns, p):
-        out = columns[:, p * pack : p * pack + 1]
-        for j in range(1, pack):
-            at = p * pack + j
-            out = jnp.where(half == j, columns[:, at : at + 1], out)
-        return jnp.broadcast_to(out, (columns.shape[0], lanes))
-
     def columns_of(g, p):
         return pl.ds(pl.multiple_of(g * gw + p * lanes, 128), lanes)
 
-    loads[4].wait()
-    loads[6].wait()
-
-    @pl.loop(0, GROUPS)
-    def _(g):
-        cum = cum_ref[pl.ds(pl.multiple_of(g * per_group, 8), per_group), :]
-        tail_t = jnp.exp(cum[:, tokens - 1 : tokens] - cum).T
-        scaled = [
-            (x_ref[:, columns_of(g, p)].astype(F32) * spread(tail_t, p)).astype(BF16)
-            for p in range(pairs)
-        ]
-        added = dot(b_ref[:, span(g, state_dim)], jnp.concatenate(scaled, axis=1), 0, 0)
-        stl_ref[g] = added
-
-        @pl.when(me == 0)
-        def _():
-            for cut in range(CUTS):
-                size = gw // CUTS
-                stout_ref[g, cut] = added[:, cut * size : (cut + 1) * size].astype(BF16)
-                stin_ref[g, cut] = jnp.zeros((state_dim, size), BF16)
-
-    @pl.when(jnp.logical_and(me == 0, has_right))
-    def _():
-        @pl.loop(0, GROUPS)
-        def _(g):
-            for cut in range(CUTS):
-                state_copy(g, cut).start()
-
-    def relay(slot):
-        k_copy, v_copy = kv_copy(slot, kbuf.at[slot], vbuf.at[slot])
-        k_copy.wait_recv()
+    def relay_key(slot):
+        copy = key_copy(slot, kbuf.at[slot])
+        copy.wait_recv()
 
         @pl.when(has_right)
         def _():
-            k_copy.start()
-
-        v_copy.wait_recv()
+            copy.start()
+
+    def relay_value(slot):
+        copy = value_copy(slot, vbuf.at[slot])
+        copy.wait_recv()
 
         @pl.when(has_right)
         def _():
-            v_copy.start()
-
-    near = lax.rem(me, 2) == 1
-
-    @pl.when(near)
-    def _():
-        relay(me - 1)
-
-    for i in (1, 2, 3):
-        loads[i].wait()
+            copy.start()
+
     visible = jnp.concatenate([(key_at <= query_at).astype(F32)] * ratio, axis=1) > 0.5
 
-    @pl.loop(0, kv_count)
-    def _(g):
+    def attend_own(g):
         for h in range(ratio):
             piece = q_ref[:, pl.ds(pl.multiple_of(g * qw + h * HEAD_SIZE, 128), HEAD_SIZE)]
             qt_ref[g, :, h * HEAD_SIZE : (h + 1) * HEAD_SIZE] = piece.T
@@ -196,31 +154,45 @@
         sum_ref[g] = jnp.sum(weight, axis=0, keepdims=True)
         acc_ref[g] = dot(vbuf[me, :, span(g, HEAD_SIZE)], weight.astype(BF16), 0, 0)
 
-    loads[5].wait()
-    loads[7].wait()
+    for load in loads[1:]:
+        load.wait()
     lower = query_at <= key_at
 
     def student_local(g):
         cum = cum_ref[pl.ds(pl.multiple_of(g * per_group, 8), per_group), :]
         cum_t = cum.T
-        reach_t = jnp.exp(cum).T
-        products = dot(c_ref[:, span(g, state_dim)], b_ref[:, span(g, state_dim)], 1, 1)
+        tail = jnp.exp(cum[:, tokens - 1 : tokens] - cum)
+        b = b_ref[:, span(g, state_dim)]
+        b_t = b.T.astype(F32)
+        products = dot(c_ref[:, span(g, state_dim)], b, 1, 1)
         for p in range(pairs):
             x = x_ref[:, columns_of(g, p)].astype(F32)
             mixes = []
+            adds = []
             sources = []
+            reach = None
             for j in range(pack):
                 h = p * pack + j
-                difference = jnp.where(lower, cum_t[:, h : h + 1] - cum[h : h + 1, :], masked_score)
+                column = jnp.broadcast_to(cum_t[:, h : h + 1], (tokens, lanes))
+                difference = jnp.where(lower, column - cum[h : h + 1, :], masked_score)
                 mixes.append((products * jnp.exp(difference)).astype(BF16))
+                adds.append((b_t * tail[h : h + 1, :]).astype(BF16))
                 sources.append(jnp.where(half == j, x, 0.0).astype(BF16))
+                reach = column if j == 0 else jnp.where(half == j, column, reach)
             z = z_ref[:, columns_of(g, p)].astype(F32)
             gate = z / (1.0 + jnp.exp(-z))
             at = slice(p * lanes, (p + 1) * lanes)
-            ssm_ref[g, :, at] = gate * dot(
-                jnp.concatenate(mixes, axis=1), jnp.concatenate(sources, axis=0)
-            )
-            reach_ref[g, :, at] = gate * spread(reach_t, p)
+            source = jnp.concatenate(sources, axis=0)
+            ssm_ref[g, :, at] = gate * dot(jnp.concatenate(mixes, axis=1), source)
+            reach_ref[g, :, at] = gate * jnp.exp(reach)
+            stl_ref[g, :, at] = dot(jnp.concatenate(adds, axis=1), source)
+
+        @pl.when(me == 0)
+        def _():
+            for cut in range(CUTS):
+                size = gw // CUTS
+                stout_ref[g, cut] = stl_ref[g, :, cut * size : (cut + 1) * size].astype(BF16)
+                stin_ref[g, cut] = jnp.zeros((state_dim, size), BF16)
 
     def attend(slot):
         @pl.loop(0, kv_count)
@@ -236,19 +208,53 @@
                 vbuf[slot, :, span(g, HEAD_SIZE)], weight.astype(BF16), 0, 0
             )
 
-    @pl.loop(0, max(n, GROUPS))
+    near = lax.rem(me, 2) == 1
+    far = jnp.logical_not(near)
+    pieces = 2 * me
+
+    @pl.loop(0, GROUPS)
     def _(r):
-        @pl.when(r < GROUPS)
-        def _():
-            student_local(r)
-
-        @pl.when(r < me)
-        def _():
-            @pl.when(jnp.logical_or(r > 0, jnp.logical_not(near)))
-            def _():
-                relay(me - 1 - r)
-
-            attend(me - 1 - r)
+        student_local(r)
+        attend_own(r)
+        piece = jnp.where(near, (r + 1) // 2, (r - 2) // 2)
+
+        @pl.when(jnp.logical_and(near, r == 0))
+        def _():
+            relay_key(me - 1)
+            relay_value(me - 1)
+
+        turn = jnp.where(near, r - 3, r - 2)
+        due = jnp.logical_and(turn >= 0, piece < pieces)
+
+        @pl.when(jnp.logical_and(due, lax.rem(turn + 4, 4) == 0))
+        def _():
+            relay_key(me - 1 - piece // 2)
+
+        @pl.when(jnp.logical_and(due, lax.rem(turn + 4, 4) == 2))
+        def _():
+            relay_value(me - 1 - piece // 2)
+
+    @pl.when(jnp.logical_and(me == 0, has_right))
+    def _():
+        @pl.loop(0, GROUPS)
+        def _(g):
+            for cut in range(CUTS):
+                state_copy(g, cut).start()
+
+    first = jnp.where(near, GROUPS // 2 + 1, GROUPS // 2 - 1)
+
+    @pl.loop(0, me)
+    def _(j):
+        attend(me - 1 - j)
+        piece = first + 2 * j
+
+        @pl.when(piece < pieces)
+        def _():
+            relay_value(me - 1 - piece // 2)
+
+        @pl.when(piece + 1 < pieces)
+        def _():
+            relay_key(me - 1 - (piece + 1) // 2)
 
     @pl.loop(0, kv_count)
     def _(g):
@@ -311,12 +317,12 @@
             for cut in range(CUTS):
                 state_copy(g, cut).wait_send()
 
-        for copy in kv_copy(me, k_hbm, v_hbm):
+        for copy in (key_copy(me, k_hbm), value_copy(me, v_hbm)):
             copy.wait_send()
 
         @pl.loop(0, me)
         def _(slot):
-            for copy in kv_copy(slot, kbuf.at[slot], vbuf.at[slot]):
+            for copy in (key_copy(slot, kbuf.at[slot]), value_copy(slot, vbuf.at[slot])):
                 copy.wait_send()
 
 

time: 56.1 us -> 55.2 us (0.984)
  Pallas kernels: 55.2 us -> 54.3 us
    pallas_call x1, Pallas kernels: 53.9 us -> 53 us  [on_device(): pl.pallas_call(functools.partial(kernel, n), out_shape=(pltpu.VMEM(studen...]
where the time goes in v3:
time: 55.2 us; the launch traced here: 54.9 us
  Pallas kernels  54.3 us (98%)
  between operations  0.64 us (1%)
    pallas_call x1, Pallas kernels, on_device(): pl.pallas_call(functools.partial(kernel, n), out_shape=(pltpu.VMEM(studen...  53 us
    pallas_call x1, Pallas kernels, on_device(): pl.pallas_call(store, out_shape=(jax.ShapeDtypeStruct(student_x.shape, BF...  1.33 us

profile of v3, /device:TPU:31, one launch (start us, length us, event | category | flops | bytes accessed | tf_op | source)
XLA Modules:
  0.0 54.9 jit_solution(10964817189244528796)
XLA Ops:
  0.6 53.0 %shard_map.113 = (bf16[128,4096]{1,0:T(8,128)(2,1)S(1)}, bf16[128,4096]{1,0:T(8,128)(2,1)S(1)}) custom-call(bf16[128,4096]{1,0:T(8,128)(2,1)} %x_hbm.1, bf16[128,4096]{1,0:T(8,128)(2,1)} %z_hbm.1, bf16[128,1024]{1,0:T(8,128)(2,1)} %b_hbm.1, bf16[128,1024]{1,0:T(8,128)(2,1)} %c_hbm.1, f32[64,128]{1,0:T(8,128)} %step_hbm.1, f32[1,64]{1,0:T(1,128)} %bitcast.3, ...), custom_call_target="tpu_custom_call" | custom-call | tf_op jit(solution)/shard_map/pallas_call | solution.py:355
  53.6 1.3 %shard_map.114 = (bf16[128,4096]{1,0:T(8,128)(2,1)}, bf16[128,4096]{1,0:T(8,128)(2,1)}) custom-call(bf16[128,4096]{1,0:T(8,128)(2,1)S(1)} %get-tuple-element.4.s_ref, bf16[128,4096]{1,0:T(8,128)(2,1)S(1)} %get-tuple-element.5.t_ref), custom_call_target="tpu_custom_call" | custom-call | tf_op jit(solution)/shard_map/pallas_call | solution.py:398

commit v4 on v3

--- a/solution.py
+++ b/solution.py
@@ -11,7 +11,7 @@
 GROUPS = 8
 HEAD_SIZE = 128
 BLOCK = 128
-CUTS = 2
+CUTS = 1
 
 epsilon_norm = 1e-05
 masked_score = -1e30

time: 55.2 us -> 53.6 us (0.971)
  Pallas kernels: 54.3 us -> 52.7 us
    pallas_call x1, Pallas kernels: 53 us -> 51.4 us  [on_device(): pl.pallas_call(functools.partial(kernel, n), out_shape=(pltpu.VMEM(studen...]
where the time goes in v4:
time: 53.6 us; the launch traced here: 53.4 us
  Pallas kernels  52.7 us (98%)
  between operations  0.64 us (1%)
    pallas_call x1, Pallas kernels, on_device(): pl.pallas_call(functools.partial(kernel, n), out_shape=(pltpu.VMEM(studen...  51.4 us
    pallas_call x1, Pallas kernels, on_device(): pl.pallas_call(store, out_shape=(jax.ShapeDtypeStruct(student_x.shape, BF...  1.33 us

profile of v4, /device:TPU:31, one launch (start us, length us, event | category | flops | bytes accessed | tf_op | source)
XLA Modules:
  0.0 53.4 jit_solution(16504413599284763715)
XLA Ops:
  0.6 51.4 %shard_map.113 = (bf16[128,4096]{1,0:T(8,128)(2,1)S(1)}, bf16[128,4096]{1,0:T(8,128)(2,1)S(1)}) custom-call(bf16[128,4096]{1,0:T(8,128)(2,1)} %x_hbm.1, bf16[128,4096]{1,0:T(8,128)(2,1)} %z_hbm.1, bf16[128,1024]{1,0:T(8,128)(2,1)} %b_hbm.1, bf16[128,1024]{1,0:T(8,128)(2,1)} %c_hbm.1, f32[64,128]{1,0:T(8,128)} %step_hbm.1, f32[1,64]{1,0:T(1,128)} %bitcast.3, ...), custom_call_target="tpu_custom_call" | custom-call | tf_op jit(solution)/shard_map/pallas_call | solution.py:355
  52.0 1.3 %shard_map.114 = (bf16[128,4096]{1,0:T(8,128)(2,1)}, bf16[128,4096]{1,0:T(8,128)(2,1)}) custom-call(bf16[128,4096]{1,0:T(8,128)(2,1)S(1)} %get-tuple-element.4.s_ref, bf16[128,4096]{1,0:T(8,128)(2,1)S(1)} %get-tuple-element.5.t_ref), custom_call_target="tpu_custom_call" | custom-call | tf_op jit(solution)/shard_map/pallas_call | solution.py:398
